TPU v7x, 32 devices: a whole 2x2x4 slice. The times are simulated.
32 devices in a mesh: parts: 2 (over y), mp: 4 (over z), shot: 4 (over x, core).
Axes of the slice: x: 2, y: 2, z: 4, core: 2. Of those that a mesh axis runs over, the one named last changes fastest.
Arguments:
- courant: float32 [192, 256, 128], P(('parts', 'mp')), parts along dimension 0, may hold values from 0.04 to 0.2
- forward_old: float32 [8, 96, 256, 128], P(('parts', 'shot'), 'mp'), parts along dimension 0, may hold values from -5 to 5
- forward_now: float32 [8, 96, 256, 128], P(('parts', 'shot'), 'mp'), parts along dimension 0, may hold values from -5 to 5
- adjoint_late: float32 [8, 96, 256, 128], P(('parts', 'shot'), 'mp'), parts along dimension 0, may hold values from -5 to 5
- adjoint_now: float32 [8, 96, 256, 128], P(('parts', 'shot'), 'mp'), parts along dimension 0, may hold values from -5 to 5
- src_cell: int32 [8, 64], P(('parts', 'shot')), parts along dimension 0, may hold values from 0 to 3145727
- src_sign: int32 [8, 64], P(('parts', 'shot')), parts along dimension 0, may hold values from 0 to 1
- wavelet: float32 [8, 2, 64], P(('parts', 'shot')), parts along dimension 0, may hold values from -16 to 16
- rec_cell: int32 [4096], P('parts'), parts along dimension 0, may hold values from 0 to 3145727
- rec_data: float32 [8, 2, 2048], P(('parts', 'shot')), parts along dimension 0, may hold values from -16 to 16
Outputs:
- raw_gradient: float32 [192, 256, 128], P(('parts', 'mp'), 'shot'), parts along dimension 0
- smooth_gradient: float32 [192, 256, 128], P(('parts', 'shot'), None, 'mp'), parts along dimension 0
There are 2 independent parts, one for each index of `parts`. A program takes and returns all parts, laid end to end along the dimension named above; each array names one. Nothing has to cross between parts.
All inputs are finite; a program needn't handle non-finite values.
Results may differ from a plain program's by a relative error of at most 0.00025.
Values sent between devices are 32-bit elements; how exact they have to be, the bound alone decides.
A program may use at most 128 MiB of HBM per device.

v0:
```python
import math

import jax
import jax.numpy as jnp
import numpy as np
from jax import lax
from jax.experimental import pallas as pl
from jax.experimental.pallas import tpu as pltpu
from jax.sharding import PartitionSpec as P

SMOOTH_X = 32
SMOOTH_YZ = 4
COEFS = (8.0 / 5.0, -1.0 / 5.0, 8.0 / 315.0, -1.0 / 560.0)
CENTER = -205.0 / 72.0
REACH = 4
HIGHEST = lax.Precision.HIGHEST
MESH = pl.DeviceIdType.MESH

SCALE = 5040.0
WHOLE = tuple(float(round(SCALE * weight)) for weight in COEFS)
MIDDLE = 3.0 * float(round(SCALE * CENTER))

VMEM = pl.BlockSpec(memory_space=pltpu.VMEM)
SMEM = pl.BlockSpec(memory_space=pltpu.SMEM)
HBM = pl.BlockSpec(memory_space=pltpu.HBM)


def smoothing_table(length, strength):
    counter = np.arange(1, length + 1, dtype=np.float64)
    sines = np.sin(np.pi * np.outer(counter, counter) / (length + 1))
    half_sine = np.sin(np.pi * counter / (2 * (length + 1)))
    resp = 1.0 / (1.0 + strength * 4.0 * half_sine**2)
    table = 2.0 / (length + 1) * (sines * resp[None, :]) @ sines
    return table, 1.0 / math.sqrt(np.mean(resp * resp))


def stencil_tables(width_y, width_z):
    def bands(length):
        return sum(
            weight * (np.eye(length, k=offset + 1) + np.eye(length, k=-offset - 1))
            for offset, weight in enumerate(WHOLE)
        )

    band_y = bands(width_y)
    band_z = np.kron(np.eye(2), bands(width_z))
    return (
        jnp.asarray(np.concatenate([band_y, band_y], axis=1), jnp.bfloat16),
        jnp.asarray(np.concatenate([band_z, band_z], axis=0), jnp.bfloat16),
    )


def split(cell, width):
    if width & (width - 1) == 0:
        return cell >> (width.bit_length() - 1), cell & (width - 1)
    return lax.div(cell, width), lax.rem(cell, width)


def inject_kernel(
    rec_cell, rec_data, src_cell, src_sign, wavelet, late, now,
    late_out, now_out, first_out, second_out, picks, sems,
):
    size = late_out.shape[0] * late_out.shape[1]
    width = late_out.shape[1]
    first = lax.axis_index("mp") * size
    copies = [
        pltpu.make_async_copy(late, late_out, sems.at[0]),
        pltpu.make_async_copy(now, now_out, sems.at[1]),
    ]
    for copy in copies:
        copy.start()
    rows = late_out.shape[0]
    step = math.gcd(rows, 64)

    def clear(index, carry):
        place = pl.ds(pl.multiple_of(index * step, step), step)
        zero = jnp.zeros((step, width), jnp.float32)
        first_out[place, :] = zero
        second_out[place, :] = zero
        return carry

    lax.fori_loop(0, rows // step, clear, 0)
    lanes = lax.broadcasted_iota(jnp.int32, (1, width), 1)

    def choose(cells):
        total = cells.shape[-1]
        together = math.gcd(total, 16)

        def some(index, count):
            for extra in range(together):
                item = index * together + extra
                local = cells[0, item] - first
                picks[count] = item
                count += jnp.where((local >= 0) & (local < size), 1, 0)
            return count

        return lax.fori_loop(0, total // together, some, 0)

    def add(cells, values, outs):
        count = choose(cells)
        group = 4

        def some(index, carry):
            places, masks, added = [], [], [[] for _ in outs]
            for extra in range(group):
                at = index * group + extra
                live = at < count
                item = jnp.where(live, picks[at], 0)
                place, lane = split(jnp.where(live, cells[0, item] - first, 0), width)
                places.append(place)
                mask = lanes == jnp.where(live, lane, -1)
                for side, value in enumerate(values(item)):
                    added[side].append(jnp.where(mask, value, 0.0))
            for side, out in enumerate(outs):
                sums = []
                for later in range(group):
                    total = added[side][later]
                    for early in range(later):
                        total += jnp.where(places[early] == places[later], added[side][early], 0.0)
                    sums.append(out[pl.ds(places[later], 1), :] + total)
                for place, total in zip(places, sums):
                    out[pl.ds(place, 1), :] = total
            return carry

        lax.fori_loop(0, lax.div(count + (group - 1), group), some, 0)

    def source_values(item):
        sign = (2 * src_sign[0, item] - 1).astype(jnp.float32)
        return sign * wavelet[0, 0, item], sign * wavelet[0, 1, item]

    add(src_cell, source_values, (first_out, second_out))
    for copy in copies:
        copy.wait()
    add(rec_cell, lambda item: (-rec_data[0, 0, item], -rec_data[0, 1, item]), (late_out, now_out))


def inject(rec_cell, rec_data, src_cell, src_sign, wavelet, late, now):
    shape = jax.ShapeDtypeStruct(late.shape, jnp.float32)
    most = max(rec_cell.shape[-1], src_cell.shape[-1])
    return pl.pallas_call(
        inject_kernel,
        out_shape=(shape,) * 4,
        in_specs=[SMEM] * 5 + [HBM] * 2,
        out_specs=(VMEM,) * 4,
        scratch_shapes=[pltpu.SMEM((most + 8,), jnp.int32), pltpu.SemaphoreType.DMA((2,))],
        compiler_params=pltpu.CompilerParams(vmem_limit_bytes=20 * 2**20),
        name="inject",
    )(rec_cell, rec_data, src_cell, src_sign, wavelet, late, now)


def slab_tables(table, count, order):
    rows = table.shape[0] // count
    mixes, sums = [], []
    for me in range(count):
        own = slice(me * rows, (me + 1) * rows)
        sums.append(np.stack([table[me * rows, own][order], table[(me + 1) * rows - 1, own][order]]))
        columns = [table[own, own][:, order]]
        for shift in range(1, count):
            source = (me - shift) % count
            seen = (source + 1) * rows - 1 if source < me else source * rows
            columns.append((table[own, seen] / table[seen, seen])[:, None])
        mixes.append(np.concatenate(columns, axis=1))
    return (
        jnp.asarray(np.stack(mixes).reshape(-1), jnp.float32),
        jnp.asarray(np.stack(sums).reshape(-1), jnp.float32),
    )


def make_kernel(slabs, groups, rows, width_y, width_z):
    blocks = rows // REACH
    chips = groups // 2
    lines = width_y // groups
    lanes = max(lines, min(128, REACH * lines))
    group = lanes // lines
    ratio = slabs // groups
    deep = width_z // slabs
    parts = ((rows - 2 * REACH) // group, 2 * REACH // group)
    starts = (0, parts[0])
    total_places = sum(parts)
    total_rows = ratio * rows
    ready_planes = slabs * total_places * deep * lanes // (width_y * width_z)

    def kernel(
        f_hbm, a_hbm, old_hbm, courant_hbm, late, now, first_source, second_source,
        table_y, table_z, smooth_y, smooth_z, mix, sums,
        raw, smooth,
        fbuf, abuf, obuf, cbuf, nbuf, mbuf, halo_one, halo_two,
        pair_in, chip_in, arrived, spread, lined, planes, planes_in,
        load_sem, one_send, one_recv, two_send, two_recv, pair_send, pair_recv,
        chip_send, chip_recv, turn_send, turn_recv, plane_send, plane_recv,
    ):
        m, s = lax.axis_index("mp"), lax.axis_index("shot")
        core = lax.rem(s, 2)
        chip = lax.div(s, 2)
        exists = (m > 0, m < slabs - 1)
        beside = (m - 1, m + 1)
        partner = s + 1 - 2 * core

        barrier = pltpu.get_barrier_semaphore()
        peers = slabs * groups
        me = m * groups + s

        def greet(index, carry):
            other = lax.rem(me + index, peers)
            pl.semaphore_signal(
                barrier, inc=1,
                device_id={"mp": lax.div(other, groups), "shot": lax.rem(other, groups)},
                device_id_type=MESH,
            )
            return carry

        lax.fori_loop(1, peers, greet, 0)

        term = abuf.reshape(rows + 2 * REACH, chips, 2, lines, width_z)
        pair = fbuf.at[: rows // 2].reshape(rows, chips, lines, width_z)
        ready = fbuf.at[rows // 2 : rows // 2 + ready_planes].reshape(slabs, total_places, deep, lanes)
        buffers = ((f_hbm, fbuf, REACH), (a_hbm, abuf, REACH), (old_hbm, obuf, 0), (courant_hbm, cbuf, 0))

        def load(which, block):
            source, target, pad = buffers[which]
            return pltpu.make_async_copy(
                source.at[pl.ds(block * REACH, REACH)],
                target.at[pl.ds(block * REACH + pad, REACH)],
                load_sem.at[which, block],
            )

        for block in range(blocks):
            for which in range(4):
                load(which, block).start()
        for buf in (fbuf, abuf, nbuf, mbuf):
            zero = jnp.zeros((REACH,) + buf.shape[1:], jnp.float32)
            buf[:REACH] = zero
            buf[REACH + rows :] = zero

        pl.semaphore_wait(barrier, peers - 1)

        def one_copy(side, field, reach):
            row = reach if side == 0 else rows - 1 - reach
            return pltpu.make_async_remote_copy(
                src_ref=(f_hbm, a_hbm)[field].at[row],
                dst_ref=halo_one.at[1 - side, field, reach],
                send_sem=one_send.at[side, field, reach],
                recv_sem=one_recv.at[1 - side, field, reach],
                device_id={"mp": beside[side]},
                device_id_type=MESH,
            )

        def two_copy(side, field, reach):
            row = reach if side == 0 else rows - 1 - reach
            return pltpu.make_async_remote_copy(
                src_ref=(nbuf, mbuf)[field].at[REACH + row],
                dst_ref=halo_two.at[1 - side, field, reach],
                send_sem=two_send.at[side, field, reach],
                recv_sem=two_recv.at[1 - side, field, reach],
                device_id={"mp": beside[side]},
                device_id_type=MESH,
            )

        def landed(buffer, sem, side, field, reach):
            ref = buffer.at[side, field, reach]
            return pltpu.make_async_copy(ref, ref, sem.at[side, field, reach])

        for side in range(2):

            @pl.when(exists[side])
            def _():
                for reach in range(REACH):
                    for field in range(2):
                        one_copy(side, field, reach).start()

        spread[...] = jnp.zeros(spread.shape, jnp.float32)
        for source in range(groups):
            for part in range(group):
                top = source * lanes + part * lines
                spread[top : top + lines, part * width_y : (part + 1) * width_y] = smooth_y[
                    source * lines : (source + 1) * lines, :
                ]

        def laplace(place, fields):
            centers = [field[place] for field in fields]
            both = jnp.concatenate(centers, axis=1)
            high = both.astype(jnp.bfloat16)
            low = (both - high.astype(jnp.float32)).astype(jnp.bfloat16)
            total = jnp.dot(
                table_y[...], jnp.concatenate([high, low], axis=0), preferred_element_type=jnp.float32
            ) + jnp.dot(
                jnp.concatenate([high, low], axis=1), table_z[...], preferred_element_type=jnp.float32
            )
            laps = []
            for side, field in enumerate(fields):
                lap = total[:, side * width_z : (side + 1) * width_z] + MIDDLE * centers[side]
                for offset, weight in enumerate(WHOLE):
                    lap += weight * (field[place + offset + 1] + field[place - offset - 1])
                laps.append(lap)
            return centers, laps

        def plane(flat, row):
            return flat[pl.ds(pl.multiple_of(row * width_y, width_y), width_y), :]

        def first_block(block, carry):
            @pl.when(block + 1 < blocks)
            def _():
                for which in range(4):
                    load(which, block + 1).wait()

            for extra in range(REACH):
                row = block * REACH + extra
                (f_row, a_row), (lap_f, lap_a) = laplace(row + REACH, (fbuf, abuf))
                here = cbuf[row] * (1.0 / SCALE)
                accel = here * lap_f + plane(first_source, row)
                nbuf[row + REACH] = (2.0 * f_row - obuf[row]) + accel
                obuf[row] = accel
                mbuf[row + REACH] = (2.0 * a_row - plane(late, row)) + here * lap_a
            return carry

        for which in range(4):
            load(which, 0).wait()
        lax.fori_loop(0, blocks, first_block, 0)

        def first_edge(reach):
            for side in range(2):

                @pl.when(exists[side])
                def _():
                    for field in range(2):
                        landed(halo_one, one_recv, side, field, reach).wait()
                    for near in range(REACH - reach):
                        row = near if side == 0 else rows - 1 - near
                        here = COEFS[reach + near] * cbuf[row]
                        add_f = here * halo_one[side, 0, reach]
                        obuf[row] += add_f
                        nbuf[row + REACH] += add_f
                        mbuf[row + REACH] += here * halo_one[side, 1, reach]
                    for field in range(2):
                        two_copy(side, field, REACH - 1 - reach).start()

        def second_block(block):
            for extra in range(REACH):
                row = block * REACH + extra
                (_, a_row), (lap_f, lap_a) = laplace(row + REACH, (nbuf, mbuf))
                here = cbuf[row] * (1.0 / SCALE)
                accel_second = here * lap_f + plane(second_source, row)
                a_first = (2.0 * a_row - plane(now, row)) + here * lap_a
                value = a_first * obuf[row] + a_row * accel_second
                term[row] = value.reshape(chips, 2, lines, width_z)

        def pair_copy(block):
            return pltpu.make_async_remote_copy(
                src_ref=term.at[pl.ds(block * REACH, REACH), :, 1 - core],
                dst_ref=pair_in.at[pl.ds(block * REACH, REACH)],
                send_sem=pair_send.at[block],
                recv_sem=pair_recv.at[block],
                device_id={"shot": partner},
                device_id_type=MESH,
            )

        def chip_copy(shift, block):
            other = lax.rem(chip + shift, chips)
            return pltpu.make_async_remote_copy(
                src_ref=pair.at[pl.ds(block * REACH, REACH), other],
                dst_ref=chip_in.at[shift - 1, pl.ds(block * REACH, REACH)],
                send_sem=chip_send.at[shift - 1, block],
                recv_sem=chip_recv.at[shift - 1, block],
                device_id={"shot": other * 2 + core},
                device_id_type=MESH,
            )

        def add_pair(block):
            pair_copy(block).wait_recv()
            here = pl.ds(block * REACH, REACH)
            pair[here] = term[here, :, core] + pair_in[here]
            for shift in range(1, chips):
                chip_copy(shift, block).start()

        def add_chips(block):
            here = pl.ds(block * REACH, REACH)
            value = pair[here, chip]
            for shift in range(1, chips):
                chip_copy(shift, block).wait_recv()
                value += chip_in[shift - 1, here]
            raw[here] = value / float(groups)

        def turn_rows(start, count, place):
            turned = lax.dot_general(
                smooth_z[...],
                raw[start : start + count].reshape(count * lines, width_z),
                (((1,), (1,)), ((), ())),
                precision=HIGHEST,
                preferred_element_type=jnp.float32,
            )
            for index in range(count // group):
                for target in range(slabs):
                    ready[target, place + index] = turned[
                        target * deep : (target + 1) * deep, index * lanes : (index + 1) * lanes
                    ]

        goal = lax.div(m, ratio)
        slot = lax.rem(m, ratio) * groups + s

        def turn_copy(part, shift):
            target = lax.rem(m + shift, slabs)
            place = pl.ds(starts[part], parts[part])
            return pltpu.make_async_remote_copy(
                src_ref=ready.at[target, place],
                dst_ref=arrived.at[slot, place],
                send_sem=turn_send.at[part, target],
                recv_sem=turn_recv.at[part, slot],
                device_id={"mp": target, "shot": goal},
                device_id_type=MESH,
            )

        def turn_start(part):
            for shift in range(1, slabs):
                turn_copy(part, shift).start()

            @pl.when(s != goal)
            def _():
                turn_copy(part, 0).start()

            @pl.when(s == goal)
            def _():
                place = pl.ds(starts[part], parts[part])
                pltpu.make_async_copy(
                    ready.at[m, place], arrived.at[slot, place], turn_recv.at[part, slot]
                ).start()

        def turn_wait(part):
            place = pl.ds(starts[part], parts[part])
            for index in range(ratio * groups):
                ref = arrived.at[index, place]
                pltpu.make_async_copy(ref, ref, turn_recv.at[part, index]).wait()

        inner = list(range(2, blocks - 2))
        near = [block for block in (1, blocks - 2) if 0 < block < blocks - 1]
        near = sorted(set(near) - set(inner))
        edges = [0, blocks - 1]

        first_edge(0)
        first_edge(1)
        for block in inner:
            second_block(block)
            pair_copy(block).start()
        first_edge(2)
        for block in inner:
            add_pair(block)
        first_edge(3)
        for block in near:
            second_block(block)
            pair_copy(block).start()
        for block in edges:
            second_block(block)
        for block in near:
            add_pair(block)
        for block in inner + near:
            add_chips(block)
        turn_rows(REACH, rows - 2 * REACH, 0)

        for reach in reversed(range(REACH)):
            for side in range(2):

                @pl.when(exists[side])
                def _():
                    for field in range(2):
                        landed(halo_two, two_recv, side, field, reach).wait()
                    for close in range(REACH - reach):
                        row = close if side == 0 else rows - 1 - close
                        here = COEFS[reach + close] * cbuf[row]
                        extra = halo_two[side, 1, reach] * obuf[row] + mbuf[row + REACH] * halo_two[side, 0, reach]
                        term[row] += (here * extra).reshape(chips, 2, lines, width_z)

        for block in edges:
            pair_copy(block).start()
        turn_start(0)
        for block in edges:
            add_pair(block)
        for block in edges:
            add_chips(block)
        turn_rows(0, REACH, parts[0])
        turn_rows(rows - REACH, REACH, parts[0] + REACH // group)
        turn_start(1)

        turn_wait(0)
        turn_wait(1)
        for index in range(ratio):
            joined = jnp.concatenate(
                [
                    arrived[index * groups + source].reshape(total_places * deep, lanes)
                    for source in range(groups)
                ],
                axis=1,
            )
            done = jnp.dot(joined, spread[...], precision=HIGHEST, preferred_element_type=jnp.float32)
            for place in range(total_places):
                for part in range(group):
                    lined[(index * total_places + place) * group + part] = done[
                        place * deep : (place + 1) * deep, part * width_y : (part + 1) * width_y
                    ]
        base = s * (2 * total_rows)
        for side in range(2):
            sum_side = sums[base + side * total_rows] * lined[0]
            for row in range(1, total_rows):
                sum_side += sums[base + side * total_rows + row] * lined[row]
            planes[side] = sum_side

        def plane_copy(shift):
            upward = jnp.where(s + shift < groups, 1, 0)
            return pltpu.make_async_remote_copy(
                src_ref=planes.at[upward],
                dst_ref=planes_in.at[shift - 1],
                send_sem=plane_send.at[shift - 1],
                recv_sem=plane_recv.at[shift - 1],
                device_id={"shot": lax.rem(s + shift, groups)},
                device_id_type=MESH,
            )

        for shift in range(1, groups):
            plane_copy(shift).start()
        for shift in range(1, groups):
            plane_copy(shift).wait_recv()
        wide = total_rows + groups - 1
        step = math.gcd(total_rows, 4)

        def mixed(index, carry):
            start = index * step
            totals = [None] * step
            for source in range(wide):
                value = lined[source] if source < total_rows else planes_in[source - total_rows]
                for extra in range(step):
                    piece = mix[(s * total_rows + start + extra) * wide + source] * value
                    totals[extra] = piece if source == 0 else totals[extra] + piece
            for extra in range(step):
                smooth[start + extra] = totals[extra]
            return carry

        lax.fori_loop(0, total_rows // step, mixed, 0)

        for side in range(2):

            @pl.when(exists[side])
            def _():
                for reach in range(REACH):
                    for field in range(2):
                        one_copy(side, field, reach).wait_send()
                        two_copy(side, field, reach).wait_send()

        for block in range(blocks):
            pair_copy(block).wait_send()
            for shift in range(1, chips):
                chip_copy(shift, block).wait_send()
        for part in range(2):
            for shift in range(1, slabs):
                turn_copy(part, shift).wait_send()

            @pl.when(s != goal)
            def _():
                turn_copy(part, 0).wait_send()

        for shift in range(1, groups):
            plane_copy(shift).wait_send()

    padded = pltpu.VMEM((rows + 2 * REACH, width_y, width_z), jnp.float32)
    slab = pltpu.VMEM((rows, width_y, width_z), jnp.float32)
    halo = pltpu.VMEM((2, 2, REACH, width_y, width_z), jnp.float32)
    dma = pltpu.SemaphoreType.DMA
    scratch = [
        padded, padded, slab, slab, padded, padded,
        halo, halo,
        pltpu.VMEM((rows, chips, lines, width_z), jnp.float32),
        pltpu.VMEM((max(1, chips - 1), rows, lines, width_z), jnp.float32),
        pltpu.VMEM((ratio * groups, total_places, deep, lanes), jnp.float32),
        pltpu.VMEM((groups * lanes, group * width_y), jnp.float32),
        pltpu.VMEM((total_rows, deep, width_y), jnp.float32),
        pltpu.VMEM((2, deep, width_y), jnp.float32),
        pltpu.VMEM((max(1, groups - 1), deep, width_y), jnp.float32),
        dma((4, blocks)),
        dma((2, 2, REACH)), dma((2, 2, REACH)), dma((2, 2, REACH)), dma((2, 2, REACH)),
        dma((blocks,)), dma((blocks,)),
        dma((max(1, chips - 1), blocks)), dma((max(1, chips - 1), blocks)),
        dma((2, slabs)), dma((2, ratio * groups)),
        dma((groups - 1,)), dma((groups - 1,)),
    ]
    outs = (
        jax.ShapeDtypeStruct((rows, lines, width_z), jnp.float32),
        jax.ShapeDtypeStruct((total_rows, deep, width_y), jnp.float32),
    )
    inner_rows = list(range(REACH, rows - REACH)) + list(range(REACH)) + list(range(rows - REACH, rows))
    order = np.concatenate([index * rows + np.array(inner_rows) for index in range(ratio)])
    return kernel, scratch, outs, order


def per_device(
    courant, forward_old, forward_now, adjoint_late, adjoint_now,
    src_cell, src_sign, wavelet, rec_cell, rec_data,
):
    rows, width_y, width_z = courant.shape
    slabs, groups = lax.axis_size("mp"), lax.axis_size("shot")
    flat = (rows * width_y, width_z)
    injected = inject(
        rec_cell.reshape(1, -1), rec_data, src_cell, src_sign, wavelet,
        adjoint_late.reshape(flat), adjoint_now.reshape(flat),
    )
    kernel, scratch, outs, order = make_kernel(slabs, groups, rows, width_y, width_z)
    table_x, spread_x = smoothing_table(rows * slabs, SMOOTH_X**2)
    smooth_y, spread_y = smoothing_table(width_y, SMOOTH_YZ**2)
    smooth_z, spread_z = smoothing_table(width_z, SMOOTH_YZ**2)
    smooth_y = smooth_y * (spread_x * spread_y * spread_z)
    raw, smooth = pl.pallas_call(
        kernel,
        out_shape=outs,
        in_specs=[HBM] * 4 + [VMEM] * 8 + [SMEM] * 2,
        out_specs=(VMEM, VMEM),
        scratch_shapes=scratch,
        compiler_params=pltpu.CompilerParams(
            collective_id=0, has_side_effects=True, vmem_limit_bytes=VMEM_GRANT
        ),
        name="gradient",
    )(
        forward_now[0], adjoint_now[0], forward_old[0], courant, *injected,
        *stencil_tables(width_y, width_z),
        jnp.asarray(smooth_y, jnp.float32), jnp.asarray(smooth_z, jnp.float32),
        *slab_tables(table_x, groups, order),
    )
    return raw, jnp.swapaxes(smooth, 1, 2)


VMEM_GRANT = 50 * 2**20


def solution(mesh):
    step = jax.shard_map(
        per_device,
        mesh=mesh,
        in_specs=(
            P(("parts", "mp"), None, None),
            P(("parts", "shot"), "mp", None, None),
            P(("parts", "shot"), "mp", None, None),
            P(("parts", "shot"), "mp", None, None),
            P(("parts", "shot"), "mp", None, None),
            P(("parts", "shot"), None),
            P(("parts", "shot"), None),
            P(("parts", "shot"), None, None),
            P("parts"),
            P(("parts", "shot"), None, None),
        ),
        out_specs=(P(("parts", "mp"), "shot", None), P(("parts", "shot"), None, "mp")),
        check_vma=False,
    )
    return step
```

profile of v0, /device:TPU:0, one launch (start us, length us, event | category | flops | bytes accessed | tf_op | source)
XLA Modules:
  0.0 114.8 jit_solution(7017381715844162746)
XLA Ops:
  0.6 0.0 copy-start
  0.6 1.9 %copy-done = f32[1,24,256,128]{3,2,1,0:T(8,128)S(1)} copy-done((f32[1,24,256,128]{3,2,1,0:T(8,128)S(1)}, f32[1,24,256,128]{3,2,1,0:T(8,128)}, u32[]{:S(2)}) %copy-start) | copy-done | bytes 3145752
  2.5 0.0 copy-start.1
  2.5 1.9 %copy-done.1 = f32[1,24,256,128]{3,2,1,0:T(8,128)S(1)} copy-done((f32[1,24,256,128]{3,2,1,0:T(8,128)S(1)}, f32[1,24,256,128]{3,2,1,0:T(8,128)}, u32[]{:S(2)}) %copy-start.1) | copy-done | bytes 3145752
  4.4 0.0 copy-start.10
  4.4 0.7 copy-done.10
  5.1 0.0 copy-start.12
  5.1 0.7 copy-done.12
  5.8 0.0 copy-start.13
  5.8 0.7 copy-done.13
  6.5 0.0 copy-start.15
  6.5 0.7 copy-done.15
  7.2 0.0 copy-start.16
  7.2 0.7 copy-done.16
  7.8 0.0 copy-start.6
  7.8 0.0 copy-start.11
  7.8 0.0 copy-start.14
  7.9 13.9 %inject.1 = (f32[6144,128]{1,0:T(8,128)S(1)}, f32[6144,128]{1,0:T(8,128)S(1)}, f32[6144,128]{1,0:T(8,128)S(1)}, f32[6144,128]{1,0:T(8,128)S(1)}) custom-call(s32[1,2048]{1,0:T(1,128)S(1)} %bitcast.11, f32[1,2,2048]{2,1,0:T(2,128)S(1)} %copy-done.10, s32[1,64]{1,0:T(1,128)S(1)} %copy-done.15, s32[1,64]{1,0:T(1,128)S(1)} %copy-done.16, ...), custom_call_target="tpu_custom_call" | custom-call | tf_op jit(solution)/shard_map/inject/pallas_call | solution.py:139
  21.8 0.0 copy-start.2
  21.8 1.6 %copy-done.2 = f32[6144,128]{1,0:T(8,128)} copy-done((f32[6144,128]{1,0:T(8,128)}, f32[6144,128]{1,0:T(8,128)S(1)}, u32[]{:S(2)}) %copy-start.2) | copy-done | bytes 3145752
  23.4 1.7 %copy-done.3 = f32[6144,128]{1,0:T(8,128)} copy-done((f32[6144,128]{1,0:T(8,128)}, f32[6144,128]{1,0:T(8,128)S(1)}, u32[]{:S(2)}) %copy-start.3) | copy-done | bytes 3145752
  25.1 1.7 %copy-done.4 = f32[6144,128]{1,0:T(8,128)} copy-done((f32[6144,128]{1,0:T(8,128)}, f32[6144,128]{1,0:T(8,128)S(1)}, u32[]{:S(2)}) %copy-start.4) | copy-done | bytes 3145752
  26.8 1.6 %copy-done.5 = f32[6144,128]{1,0:T(8,128)} copy-done((f32[6144,128]{1,0:T(8,128)}, f32[6144,128]{1,0:T(8,128)S(1)}, u32[]{:S(2)}) %copy-start.5) | copy-done | bytes 3145752
  28.5 0.0 copy-done.6
  28.5 0.0 copy-done.7
  28.5 0.0 copy-done.8
  28.5 0.0 copy-done.9
  28.5 0.0 copy-done.11
  28.5 0.0 copy-done.14
  28.5 84.5 %gradient.1 = (f32[24,64,128]{2,1,0:T(8,128)S(1)}, f32[24,32,256]{2,1,0:T(8,128)S(1)}) custom-call(f32[24,256,128]{2,1,0:T(8,128)} %bitcast.12, f32[24,256,128]{2,1,0:T(8,128)} %bitcast.7, f32[24,256,128]{2,1,0:T(8,128)} %bitcast.13, f32[24,256,128]{2,1,0:T(8,128)} %courant_hbm.1, f32[6144,128]{1,0:T(8,128)} %copy-done.2, f32[6144,128]{1,0:T(8,128)} %copy-done.3, ...), custom_call_target="tpu_custom_call" | custom-call | tf_op jit(solution)/shard_map/gradient/pallas_call | solution.py:606
  113.0 0.9 copy.20
  113.9 0.9 copy.21
  (6 shorter events, 0.0 us)
Async XLA Ops:
  0.6 1.9 %copy-start = (f32[1,24,256,128]{3,2,1,0:T(8,128)S(1)}, f32[1,24,256,128]{3,2,1,0:T(8,128)}, u32[]{:S(2)}) copy-start(f32[1,24,256,128]{3,2,1,0:T(8,128)} %param.20) | copy-start | bytes 9437188
  2.5 1.9 %copy-start.1 = (f32[1,24,256,128]{3,2,1,0:T(8,128)S(1)}, f32[1,24,256,128]{3,2,1,0:T(8,128)}, u32[]{:S(2)}) copy-start(f32[1,24,256,128]{3,2,1,0:T(8,128)} %param.19) | copy-start | bytes 9437188
  4.4 0.7 copy-start.10
  5.1 0.7 copy-start.12
  5.8 0.7 copy-start.13
  6.5 0.7 copy-start.15
  7.2 0.7 copy-start.16
  7.8 20.6 %copy-start.6 = (f32[256,256]{1,0:T(8,128)S(1)}, f32[256,256]{1,0:T(8,128)}, u32[]{:S(2)}) copy-start(f32[256,256]{1,0:T(8,128)} %constant.14.clone.smooth_y) | copy-start | bytes 786436
  7.8 20.6 %copy-start.7 = (bf16[512,256]{1,0:T(8,128)(2,1)S(1)}, bf16[512,256]{1,0:T(8,128)(2,1)}, u32[]{:S(2)}) copy-start(bf16[512,256]{1,0:T(8,128)(2,1)} %constant.13.clone.table_z) | copy-start | bytes 786436
  7.8 20.6 %copy-start.8 = (bf16[256,512]{1,0:T(8,128)(2,1)S(1)}, bf16[256,512]{1,0:T(8,128)(2,1)}, u32[]{:S(2)}) copy-start(bf16[256,512]{1,0:T(8,128)(2,1)} %constant.12.clone.table_y) | copy-start | bytes 786436
  7.8 20.6 %copy-start.9 = (f32[128,128]{1,0:T(8,128)S(1)}, f32[128,128]{1,0:T(8,128)}, u32[]{:S(2)}) copy-start(f32[128,128]{1,0:T(8,128)} %constant.15.clone.smooth_z) | copy-start | bytes 196612
  7.8 20.6 %copy-start.11 = (f32[2592]{0:T(1024)S(1)}, f32[2592]{0:T(1024)}, u32[]{:S(2)}) copy-start(f32[2592]{0:T(1024)} %constant.16.clone.mix) | copy-start | bytes 31108
  7.8 20.6 %copy-start.14 = (f32[192]{0:T(256)S(1)}, f32[192]{0:T(256)}, u32[]{:S(2)}) copy-start(f32[192]{0:T(256)} %constant.17.clone.sums) | copy-start | bytes 2308
  21.8 1.6 %copy-start.2 = (f32[6144,128]{1,0:T(8,128)}, f32[6144,128]{1,0:T(8,128)S(1)}, u32[]{:S(2)}) copy-start(f32[6144,128]{1,0:T(8,128)S(1)} %get-tuple-element.8.late) | copy-start | bytes 9437188
  23.4 1.7 %copy-start.3 = (f32[6144,128]{1,0:T(8,128)}, f32[6144,128]{1,0:T(8,128)S(1)}, u32[]{:S(2)}) copy-start(f32[6144,128]{1,0:T(8,128)S(1)} %get-tuple-element.9.now) | copy-start | bytes 9437188
  25.1 1.7 %copy-start.4 = (f32[6144,128]{1,0:T(8,128)}, f32[6144,128]{1,0:T(8,128)S(1)}, u32[]{:S(2)}) copy-start(f32[6144,128]{1,0:T(8,128)S(1)} %get-tuple-element.10.first_source) | copy-start | bytes 9437188
  26.8 1.7 %copy-start.5 = (f32[6144,128]{1,0:T(8,128)}, f32[6144,128]{1,0:T(8,128)S(1)}, u32[]{:S(2)}) copy-start(f32[6144,128]{1,0:T(8,128)S(1)} %get-tuple-element.11.second_source) | copy-start | bytes 9437188
where the time goes:
time: 115 us
  Pallas kernels  98.4 us (86%)
  local copies, waits for them, and re-layouts  15.6 us (14%)
    pallas_call x1, Pallas kernels, per_device(): pl.pallas_call(kernel, out_shape=outs, in_specs=[HBM] * 4 + [VMEM] * 8 +...  84.5 us
    unnamed x36, local copies, waits for them, and re-layouts  15.6 us
    pallas_call x1, Pallas kernels, inject(): pl.pallas_call(inject_kernel, out_shape=(shape,) * 4, in_specs=[SMEM] * 5...  13.9 us

commit v1 on v0

--- a/solution.py
+++ b/solution.py
@@ -57,66 +57,74 @@
 
 def inject_kernel(
     rec_cell, rec_data, src_cell, src_sign, wavelet, late, now,
-    late_out, now_out, first_out, second_out, picks, sems,
+    late_out, now_out, first_out, second_out,
+    late_buf, now_buf, first_buf, second_buf,
+    rec_cells, rec_values, src_cells, src_signs, src_values, picks, sems,
 ):
-    size = late_out.shape[0] * late_out.shape[1]
-    width = late_out.shape[1]
+    rows, width = late_buf.shape
+    size = rows * width
     first = lax.axis_index("mp") * size
+    moves = [
+        (rec_cell, rec_cells), (rec_data, rec_values), (src_cell, src_cells),
+        (src_sign, src_signs), (wavelet, src_values), (late, late_buf), (now, now_buf),
+        (first_buf, first_out), (second_buf, second_out), (late_buf, late_out), (now_buf, now_out),
+    ]
     copies = [
-        pltpu.make_async_copy(late, late_out, sems.at[0]),
-        pltpu.make_async_copy(now, now_out, sems.at[1]),
+        pltpu.make_async_copy(source, target, sems.at[index])
+        for index, (source, target) in enumerate(moves)
     ]
-    for copy in copies:
+    for copy in copies[:7]:
         copy.start()
-    rows = late_out.shape[0]
     step = math.gcd(rows, 64)
 
     def clear(index, carry):
         place = pl.ds(pl.multiple_of(index * step, step), step)
         zero = jnp.zeros((step, width), jnp.float32)
-        first_out[place, :] = zero
-        second_out[place, :] = zero
+        first_buf[place, :] = zero
+        second_buf[place, :] = zero
         return carry
 
     lax.fori_loop(0, rows // step, clear, 0)
     lanes = lax.broadcasted_iota(jnp.int32, (1, width), 1)
 
-    def choose(cells):
-        total = cells.shape[-1]
+    def choose(load, total):
         together = math.gcd(total, 16)
 
         def some(index, count):
-            for extra in range(together):
-                item = index * together + extra
-                local = cells[0, item] - first
+            items = [index * together + extra for extra in range(together)]
+            locals_ = [load(item) - first for item in items]
+            valid = [jnp.where((local >= 0) & (local < size), 1, 0) for local in locals_]
+            for item, ok in zip(items, valid):
                 picks[count] = item
-                count += jnp.where((local >= 0) & (local < size), 1, 0)
+                count += ok
             return count
 
         return lax.fori_loop(0, total // together, some, 0)
 
-    def add(cells, values, outs):
-        count = choose(cells)
+    def add(count, load, values, outs):
         group = 4
 
         def some(index, carry):
-            places, masks, added = [], [], [[] for _ in outs]
-            for extra in range(group):
-                at = index * group + extra
-                live = at < count
-                item = jnp.where(live, picks[at], 0)
-                place, lane = split(jnp.where(live, cells[0, item] - first, 0), width)
+            ats = [index * group + extra for extra in range(group)]
+            lives = [at < count for at in ats]
+            items = [jnp.where(live, picks[at], 0) for at, live in zip(ats, lives)]
+            cells = [load(item) - first for item in items]
+            amounts = [values(item) for item in items]
+            places, added = [], [[] for _ in outs]
+            for cell, live, amount in zip(cells, lives, amounts):
+                place, lane = split(jnp.where(live, cell, 0), width)
                 places.append(place)
                 mask = lanes == jnp.where(live, lane, -1)
-                for side, value in enumerate(values(item)):
+                for side, value in enumerate(amount):
                     added[side].append(jnp.where(mask, value, 0.0))
+            olds = [[out[pl.ds(place, 1), :] for place in places] for out in outs]
             for side, out in enumerate(outs):
                 sums = []
                 for later in range(group):
                     total = added[side][later]
                     for early in range(later):
                         total += jnp.where(places[early] == places[later], added[side][early], 0.0)
-                    sums.append(out[pl.ds(places[later], 1), :] + total)
+                    sums.append(olds[side][later] + total)
                 for place, total in zip(places, sums):
                     out[pl.ds(place, 1), :] = total
             return carry
@@ -124,27 +132,43 @@
         lax.fori_loop(0, lax.div(count + (group - 1), group), some, 0)
 
     def source_values(item):
-        sign = (2 * src_sign[0, item] - 1).astype(jnp.float32)
-        return sign * wavelet[0, 0, item], sign * wavelet[0, 1, item]
-
-    add(src_cell, source_values, (first_out, second_out))
-    for copy in copies:
+        sign = (2 * src_signs[0, item] - 1).astype(jnp.float32)
+        return sign * src_values[0, 0, item], sign * src_values[0, 1, item]
+
+    for copy in copies[:5]:
         copy.wait()
-    add(rec_cell, lambda item: (-rec_data[0, 0, item], -rec_data[0, 1, item]), (late_out, now_out))
+    count = choose(lambda item: src_cells[0, item], src_cells.shape[1])
+    add(count, lambda item: src_cells[0, item], source_values, (first_buf, second_buf))
+    copies[7].start()
+    copies[8].start()
+    count = choose(lambda item: rec_cells[item], rec_cells.shape[0])
+    copies[5].wait()
+    copies[6].wait()
+    add(
+        count, lambda item: rec_cells[item],
+        lambda item: (-rec_values[0, 0, item], -rec_values[0, 1, item]), (late_buf, now_buf),
+    )
+    copies[9].start()
+    copies[10].start()
+    for copy in copies[7:]:
+        copy.wait()
 
 
 def inject(rec_cell, rec_data, src_cell, src_sign, wavelet, late, now):
     shape = jax.ShapeDtypeStruct(late.shape, jnp.float32)
     most = max(rec_cell.shape[-1], src_cell.shape[-1])
+    small = (rec_cell, rec_data, src_cell, src_sign, wavelet)
     return pl.pallas_call(
         inject_kernel,
         out_shape=(shape,) * 4,
-        in_specs=[SMEM] * 5 + [HBM] * 2,
-        out_specs=(VMEM,) * 4,
-        scratch_shapes=[pltpu.SMEM((most + 8,), jnp.int32), pltpu.SemaphoreType.DMA((2,))],
-        compiler_params=pltpu.CompilerParams(vmem_limit_bytes=20 * 2**20),
+        in_specs=[HBM] * 7,
+        out_specs=(HBM,) * 4,
+        scratch_shapes=[pltpu.VMEM(late.shape, jnp.float32)] * 4
+        + [pltpu.SMEM(array.shape, array.dtype) for array in small]
+        + [pltpu.SMEM((most + 8,), jnp.int32), pltpu.SemaphoreType.DMA((11,))],
+        compiler_params=pltpu.CompilerParams(vmem_limit_bytes=VMEM_GRANT),
         name="inject",
-    )(rec_cell, rec_data, src_cell, src_sign, wavelet, late, now)
+    )(*small, late, now)
 
 
 def slab_tables(table, count, order):
@@ -180,11 +204,11 @@
     ready_planes = slabs * total_places * deep * lanes // (width_y * width_z)
 
     def kernel(
-        f_hbm, a_hbm, old_hbm, courant_hbm, late, now, first_source, second_source,
-        table_y, table_z, smooth_y, smooth_z, mix, sums,
-        raw, smooth,
-        fbuf, abuf, obuf, cbuf, nbuf, mbuf, halo_one, halo_two,
-        pair_in, chip_in, arrived, spread, lined, planes, planes_in,
+        f_hbm, a_hbm, old_hbm, courant_hbm, late_hbm, now_hbm, first_hbm, second_hbm,
+        table_y, table_z, smooth_y, smooth_z, sums,
+        raw_out, lined, planes_in,
+        raw, fbuf, abuf, obuf, cbuf, nbuf, mbuf, lbuf, sbuf, halo_one, halo_two,
+        pair_in, chip_in, arrived, spread, planes,
         load_sem, one_send, one_recv, two_send, two_recv, pair_send, pair_recv,
         chip_send, chip_recv, turn_send, turn_recv, plane_send, plane_recv,
     ):
@@ -195,6 +219,11 @@
         beside = (m - 1, m + 1)
         partner = s + 1 - 2 * core
 
+        inner = list(range(2, blocks - 2))
+        near = [block for block in (1, blocks - 2) if 0 < block < blocks - 1]
+        near = sorted(set(near) - set(inner))
+        edges = [0, blocks - 1]
+
         barrier = pltpu.get_barrier_semaphore()
         peers = slabs * groups
         me = m * groups + s
@@ -213,7 +242,10 @@
         term = abuf.reshape(rows + 2 * REACH, chips, 2, lines, width_z)
         pair = fbuf.at[: rows // 2].reshape(rows, chips, lines, width_z)
         ready = fbuf.at[rows // 2 : rows // 2 + ready_planes].reshape(slabs, total_places, deep, lanes)
-        buffers = ((f_hbm, fbuf, REACH), (a_hbm, abuf, REACH), (old_hbm, obuf, 0), (courant_hbm, cbuf, 0))
+        buffers = (
+            (f_hbm, fbuf, REACH), (a_hbm, abuf, REACH), (old_hbm, obuf, 0), (courant_hbm, cbuf, 0),
+            (late_hbm, lbuf, 0), (first_hbm, sbuf, 0), (now_hbm, lbuf, 0), (second_hbm, sbuf, 0),
+        )
 
         def load(which, block):
             source, target, pad = buffers[which]
@@ -224,7 +256,7 @@
             )
 
         for block in range(blocks):
-            for which in range(4):
+            for which in range(6):
                 load(which, block).start()
         for buf in (fbuf, abuf, nbuf, mbuf):
             zero = jnp.zeros((REACH,) + buf.shape[1:], jnp.float32)
@@ -293,28 +325,28 @@
                 laps.append(lap)
             return centers, laps
 
-        def plane(flat, row):
-            return flat[pl.ds(pl.multiple_of(row * width_y, width_y), width_y), :]
-
         def first_block(block, carry):
             @pl.when(block + 1 < blocks)
             def _():
-                for which in range(4):
+                for which in range(6):
                     load(which, block + 1).wait()
 
             for extra in range(REACH):
                 row = block * REACH + extra
                 (f_row, a_row), (lap_f, lap_a) = laplace(row + REACH, (fbuf, abuf))
                 here = cbuf[row] * (1.0 / SCALE)
-                accel = here * lap_f + plane(first_source, row)
+                accel = here * lap_f + sbuf[row]
                 nbuf[row + REACH] = (2.0 * f_row - obuf[row]) + accel
                 obuf[row] = accel
-                mbuf[row + REACH] = (2.0 * a_row - plane(late, row)) + here * lap_a
+                mbuf[row + REACH] = (2.0 * a_row - lbuf[row]) + here * lap_a
             return carry
 
-        for which in range(4):
+        for which in range(6):
             load(which, 0).wait()
         lax.fori_loop(0, blocks, first_block, 0)
+        for block in inner + near + edges:
+            for which in (6, 7):
+                load(which, block).start()
 
         def first_edge(reach):
             for side in range(2):
@@ -334,12 +366,14 @@
                         two_copy(side, field, REACH - 1 - reach).start()
 
         def second_block(block):
+            for which in (6, 7):
+                load(which, block).wait()
             for extra in range(REACH):
                 row = block * REACH + extra
                 (_, a_row), (lap_f, lap_a) = laplace(row + REACH, (nbuf, mbuf))
                 here = cbuf[row] * (1.0 / SCALE)
-                accel_second = here * lap_f + plane(second_source, row)
-                a_first = (2.0 * a_row - plane(now, row)) + here * lap_a
+                accel_second = here * lap_f + sbuf[row]
+                a_first = (2.0 * a_row - lbuf[row]) + here * lap_a
                 value = a_first * obuf[row] + a_row * accel_second
                 term[row] = value.reshape(chips, 2, lines, width_z)
 
@@ -428,11 +462,6 @@
             for index in range(ratio * groups):
                 ref = arrived.at[index, place]
                 pltpu.make_async_copy(ref, ref, turn_recv.at[part, index]).wait()
-
-        inner = list(range(2, blocks - 2))
-        near = [block for block in (1, blocks - 2) if 0 < block < blocks - 1]
-        near = sorted(set(near) - set(inner))
-        edges = [0, blocks - 1]
 
         first_edge(0)
         first_edge(1)
@@ -477,6 +506,8 @@
         turn_rows(0, REACH, parts[0])
         turn_rows(rows - REACH, REACH, parts[0] + REACH // group)
         turn_start(1)
+        raw_copy = pltpu.make_async_copy(raw, raw_out, load_sem.at[0, 0])
+        raw_copy.start()
 
         turn_wait(0)
         turn_wait(1)
@@ -516,23 +547,6 @@
             plane_copy(shift).start()
         for shift in range(1, groups):
             plane_copy(shift).wait_recv()
-        wide = total_rows + groups - 1
-        step = math.gcd(total_rows, 4)
-
-        def mixed(index, carry):
-            start = index * step
-            totals = [None] * step
-            for source in range(wide):
-                value = lined[source] if source < total_rows else planes_in[source - total_rows]
-                for extra in range(step):
-                    piece = mix[(s * total_rows + start + extra) * wide + source] * value
-                    totals[extra] = piece if source == 0 else totals[extra] + piece
-            for extra in range(step):
-                smooth[start + extra] = totals[extra]
-            return carry
-
-        lax.fori_loop(0, total_rows // step, mixed, 0)
-
         for side in range(2):
 
             @pl.when(exists[side])
@@ -556,22 +570,22 @@
 
         for shift in range(1, groups):
             plane_copy(shift).wait_send()
+        raw_copy.wait()
 
     padded = pltpu.VMEM((rows + 2 * REACH, width_y, width_z), jnp.float32)
     slab = pltpu.VMEM((rows, width_y, width_z), jnp.float32)
     halo = pltpu.VMEM((2, 2, REACH, width_y, width_z), jnp.float32)
     dma = pltpu.SemaphoreType.DMA
     scratch = [
-        padded, padded, slab, slab, padded, padded,
+        pltpu.VMEM((rows, lines, width_z), jnp.float32),
+        padded, padded, slab, slab, padded, padded, slab, slab,
         halo, halo,
         pltpu.VMEM((rows, chips, lines, width_z), jnp.float32),
         pltpu.VMEM((max(1, chips - 1), rows, lines, width_z), jnp.float32),
         pltpu.VMEM((ratio * groups, total_places, deep, lanes), jnp.float32),
         pltpu.VMEM((groups * lanes, group * width_y), jnp.float32),
-        pltpu.VMEM((total_rows, deep, width_y), jnp.float32),
         pltpu.VMEM((2, deep, width_y), jnp.float32),
-        pltpu.VMEM((max(1, groups - 1), deep, width_y), jnp.float32),
-        dma((4, blocks)),
+        dma((8, blocks)),
         dma((2, 2, REACH)), dma((2, 2, REACH)), dma((2, 2, REACH)), dma((2, 2, REACH)),
         dma((blocks,)), dma((blocks,)),
         dma((max(1, chips - 1), blocks)), dma((max(1, chips - 1), blocks)),
@@ -581,10 +595,72 @@
     outs = (
         jax.ShapeDtypeStruct((rows, lines, width_z), jnp.float32),
         jax.ShapeDtypeStruct((total_rows, deep, width_y), jnp.float32),
+        jax.ShapeDtypeStruct((groups - 1, deep, width_y), jnp.float32),
     )
     inner_rows = list(range(REACH, rows - REACH)) + list(range(REACH)) + list(range(rows - REACH, rows))
     order = np.concatenate([index * rows + np.array(inner_rows) for index in range(ratio)])
     return kernel, scratch, outs, order
+
+
+def mix_kernel(
+    raw_hbm, lined_hbm, planes_hbm, mix, raw_out, smooth, raw, lined, planes, buffer, sems
+):
+    total_rows, others = lined.shape[0], planes.shape[0]
+    wide = total_rows + others
+    step = math.gcd(total_rows, 4)
+    base = lax.axis_index("shot") * total_rows
+    copies = [
+        pltpu.make_async_copy(source, target, sems.at[index])
+        for index, (source, target) in enumerate(
+            [(lined_hbm, lined), (planes_hbm, planes), (raw_hbm, raw), (raw, raw_out)]
+        )
+    ]
+    for copy in copies[:3]:
+        copy.start()
+    for copy in copies[:3]:
+        copy.wait()
+    copies[3].start()
+
+    def write(index):
+        here = pl.ds(index * step, step)
+        return pltpu.make_async_copy(buffer.at[here], smooth.at[here], sems.at[index + 4])
+
+    def some(index, carry):
+        totals = [None] * step
+        for source in range(wide):
+            value = lined[source] if source < total_rows else planes[source - total_rows]
+            for extra in range(step):
+                piece = mix[(base + index * step + extra) * wide + source] * value
+                totals[extra] = piece if source == 0 else totals[extra] + piece
+        for extra in range(step):
+            buffer[index * step + extra] = totals[extra]
+        write(index).start()
+        return carry
+
+    lax.fori_loop(0, total_rows // step, some, 0)
+    for index in range(total_rows // step):
+        write(index).wait()
+    copies[3].wait()
+
+
+def mix_planes(raw, lined, planes, mix):
+    steps = lined.shape[0] // math.gcd(lined.shape[0], 4)
+    return pl.pallas_call(
+        mix_kernel,
+        out_shape=(
+            jax.ShapeDtypeStruct(raw.shape, jnp.float32),
+            jax.ShapeDtypeStruct(lined.shape, jnp.float32),
+        ),
+        in_specs=[HBM, HBM, HBM, SMEM],
+        out_specs=(HBM, HBM),
+        scratch_shapes=[
+            pltpu.VMEM(raw.shape, jnp.float32), pltpu.VMEM(lined.shape, jnp.float32),
+            pltpu.VMEM(planes.shape, jnp.float32), pltpu.VMEM(lined.shape, jnp.float32),
+            pltpu.SemaphoreType.DMA((steps + 4,)),
+        ],
+        compiler_params=pltpu.CompilerParams(vmem_limit_bytes=VMEM_GRANT),
+        name="mix",
+    )(raw, lined, planes, mix)
 
 
 def per_device(
@@ -595,7 +671,7 @@
     slabs, groups = lax.axis_size("mp"), lax.axis_size("shot")
     flat = (rows * width_y, width_z)
     injected = inject(
-        rec_cell.reshape(1, -1), rec_data, src_cell, src_sign, wavelet,
+        rec_cell, rec_data, src_cell, src_sign, wavelet,
         adjoint_late.reshape(flat), adjoint_now.reshape(flat),
     )
     kernel, scratch, outs, order = make_kernel(slabs, groups, rows, width_y, width_z)
@@ -603,26 +679,30 @@
     smooth_y, spread_y = smoothing_table(width_y, SMOOTH_YZ**2)
     smooth_z, spread_z = smoothing_table(width_z, SMOOTH_YZ**2)
     smooth_y = smooth_y * (spread_x * spread_y * spread_z)
-    raw, smooth = pl.pallas_call(
+    mix, sums = slab_tables(table_x, groups, order)
+    raw, lined, planes = pl.pallas_call(
         kernel,
         out_shape=outs,
-        in_specs=[HBM] * 4 + [VMEM] * 8 + [SMEM] * 2,
-        out_specs=(VMEM, VMEM),
+        in_specs=[HBM] * 8 + [VMEM] * 4 + [SMEM],
+        out_specs=(HBM, VMEM, VMEM),
         scratch_shapes=scratch,
         compiler_params=pltpu.CompilerParams(
-            collective_id=0, has_side_effects=True, vmem_limit_bytes=VMEM_GRANT
+            collective_id=0, has_side_effects=True, vmem_limit_bytes=GRADIENT_GRANT
         ),
         name="gradient",
     )(
-        forward_now[0], adjoint_now[0], forward_old[0], courant, *injected,
+        forward_now[0], adjoint_now[0], forward_old[0], courant,
+        *(array.reshape(rows, width_y, width_z) for array in injected),
         *stencil_tables(width_y, width_z),
         jnp.asarray(smooth_y, jnp.float32), jnp.asarray(smooth_z, jnp.float32),
-        *slab_tables(table_x, groups, order),
+        sums,
     )
+    raw, smooth = mix_planes(raw, lined, planes, mix)
     return raw, jnp.swapaxes(smooth, 1, 2)
 
 
-VMEM_GRANT = 50 * 2**20
+VMEM_GRANT = 60 * 2**20
+GRADIENT_GRANT = 56 * 2**20
 
 
 def solution(mesh):

time: 115 us -> 103 us (0.90)
  local copies, waits for them, and re-layouts: 15.6 us -> 0 us
  Pallas kernels: 98.4 us -> 102 us
    unnamed x36 -> x0, local copies, waits for them, and re-layouts: 15.6 us -> none
    pallas_call x2 -> x3, Pallas kernels: 98.4 us -> 102 us  [the longest x1 80.6 us: per_device(): pl.pallas_call(kernel, out_shape=outs, in_specs=[HBM] * 8 + [VMEM] * 4 +...]
where the time goes in v1:
time: 103 us
  Pallas kernels  102 us (99%)
    pallas_call x1, Pallas kernels, per_device(): pl.pallas_call(kernel, out_shape=outs, in_specs=[HBM] * 8 + [VMEM] * 4 +...  80.6 us
    pallas_call x1, Pallas kernels, inject(): pl.pallas_call(inject_kernel, out_shape=(shape,) * 4, in_specs=[HBM] * 7,...  17.1 us
    pallas_call x1, Pallas kernels, mix_planes(): pl.pallas_call(mix_kernel, out_shape=(jax.ShapeDtypeStruct(raw.shape, jnp...  4.55 us

profile of v1, /device:TPU:0, one launch (start us, length us, event | category | flops | bytes accessed | tf_op | source)
XLA Modules:
  0.0 103.1 jit_solution(9026940386687053737)
XLA Ops:
  0.6 17.1 %inject.1 = (f32[6144,128]{1,0:T(8,128)}, f32[6144,128]{1,0:T(8,128)}, f32[6144,128]{1,0:T(8,128)}, f32[6144,128]{1,0:T(8,128)}) custom-call(s32[2048]{0:T(1024)} %rec_cell.1, f32[1,2,2048]{2,1,0:T(2,128)} %rec_data.1, s32[1,64]{1,0:T(1,128)} %src_cell.1, s32[1,64]{1,0:T(1,128)} %src_sign.1, f32[1,2,64]{2,1,0:T(2,128)} %wavelet.1, f32[6144,128]{1,0:T(8,128)} %bitcast.18, ...), custom_call_target="tpu_custom_call" | custom-call | tf_op jit(solution)/shard_map/inject/pallas_call | solution.py:161
  17.8 80.6 %gradient.1 = (f32[24,64,128]{2,1,0:T(8,128)}, f32[24,32,256]{2,1,0:T(8,128)}, f32[3,32,256]{2,1,0:T(8,128)}) custom-call(f32[24,256,128]{2,1,0:T(8,128)} %bitcast.12, f32[24,256,128]{2,1,0:T(8,128)} %bitcast.11, f32[24,256,128]{2,1,0:T(8,128)} %bitcast.13, f32[24,256,128]{2,1,0:T(8,128)} %courant_hbm.1, f32[24,256,128]{2,1,0:T(8,128)} %bitcast.14, ...), custom_call_target="tpu_custom_call" | custom-call | tf_op jit(solution)/shard_map/gradient/pallas_call | solution.py:683
  98.4 4.5 %mix.2 = (f32[24,64,128]{2,1,0:T(8,128)}, f32[24,32,256]{2,1,0:T(8,128)}) custom-call(f32[24,64,128]{2,1,0:T(8,128)} %get-tuple-element.15.raw_hbm, f32[24,32,256]{2,1,0:T(8,128)} %get-tuple-element.16.lined_hbm, f32[3,32,256]{2,1,0:T(8,128)} %get-tuple-element.17.planes_hbm, f32[2592]{0:T(1024)} %constant.12.clone.mix), custom_call_target="tpu_custom_call" | custom-call | tf_op jit(solution)/shard_map/mix/pallas_call | solution.py:648

commit v2 on v1

--- a/solution.py
+++ b/solution.py
@@ -56,26 +56,28 @@
 
 
 def inject_kernel(
-    rec_cell, rec_data, src_cell, src_sign, wavelet, late, now,
+    packed, rec_data, src_sign, wavelet, late, now,
     late_out, now_out, first_out, second_out,
     late_buf, now_buf, first_buf, second_buf,
-    rec_cells, rec_values, src_cells, src_signs, src_values, picks, sems,
+    cells, rec_values, src_signs, src_values, picks, sems,
 ):
-    rows, width = late_buf.shape
-    size = rows * width
-    first = lax.axis_index("mp") * size
+    size, width = math.prod(late.shape), late.shape[1]
+    rows = size // width
+    bits = cell_bits(size, width)
+    whole = pl.ds(0, rows)
     moves = [
-        (rec_cell, rec_cells), (rec_data, rec_values), (src_cell, src_cells),
-        (src_sign, src_signs), (wavelet, src_values), (late, late_buf), (now, now_buf),
-        (first_buf, first_out), (second_buf, second_out), (late_buf, late_out), (now_buf, now_out),
+        (packed, cells), (rec_data, rec_values), (src_sign, src_signs), (wavelet, src_values),
+        (late, late_buf.at[whole]), (now, now_buf.at[whole]),
+        (first_buf.at[whole], first_out), (second_buf.at[whole], second_out),
+        (late_buf.at[whole], late_out), (now_buf.at[whole], now_out),
     ]
     copies = [
         pltpu.make_async_copy(source, target, sems.at[index])
         for index, (source, target) in enumerate(moves)
     ]
-    for copy in copies[:7]:
+    for copy in copies[:6]:
         copy.start()
-    step = math.gcd(rows, 64)
+    step = math.gcd(rows, 256)
 
     def clear(index, carry):
         place = pl.ds(pl.multiple_of(index * step, step), step)
@@ -86,86 +88,100 @@
 
     lax.fori_loop(0, rows // step, clear, 0)
     lanes = lax.broadcasted_iota(jnp.int32, (1, width), 1)
-
-    def choose(load, total):
-        together = math.gcd(total, 16)
+    group = GROUP
+
+    def choose(start, total):
+        together = math.gcd(total, 32)
 
         def some(index, count):
-            items = [index * together + extra for extra in range(together)]
-            locals_ = [load(item) - first for item in items]
-            valid = [jnp.where((local >= 0) & (local < size), 1, 0) for local in locals_]
-            for item, ok in zip(items, valid):
-                picks[count] = item
-                count += ok
+            values = [cells[start + index * together + extra] for extra in range(together)]
+            grows = [1 + (value >> 31) for value in values]
+            for value, grow in zip(values, grows):
+                picks[count] = value
+                count += grow
             return count
 
-        return lax.fori_loop(0, total // together, some, 0)
-
-    def add(count, load, values, outs):
-        group = 4
+        count = lax.fori_loop(0, total // together, some, 0)
+        for extra in range(2 * group - 1):
+            picks[count + extra] = size
+        return count
+
+    def add(count, amounts, outs, sign):
+        def fetch(index):
+            values = [picks[index * group + extra] for extra in range(group)]
+            amount = tuple(amounts(value >> bits) for value in values)
+            local = [value & ((1 << bits) - 1) for value in values]
+            return tuple(split(cell, width) for cell in local), amount
 
         def some(index, carry):
-            ats = [index * group + extra for extra in range(group)]
-            lives = [at < count for at in ats]
-            items = [jnp.where(live, picks[at], 0) for at, live in zip(ats, lives)]
-            cells = [load(item) - first for item in items]
-            amounts = [values(item) for item in items]
-            places, added = [], [[] for _ in outs]
-            for cell, live, amount in zip(cells, lives, amounts):
-                place, lane = split(jnp.where(live, cell, 0), width)
-                places.append(place)
-                mask = lanes == jnp.where(live, lane, -1)
-                for side, value in enumerate(amount):
-                    added[side].append(jnp.where(mask, value, 0.0))
+            spots, amount = carry
+            places, lane = zip(*spots)
             olds = [[out[pl.ds(place, 1), :] for place in places] for out in outs]
+            masks = [lanes == column for column in lane]
+            added = [
+                [jnp.where(mask, pair[side], 0.0) for mask, pair in zip(masks, amount)]
+                for side in range(len(outs))
+            ]
+            totals = [list(parts) for parts in added]
+            for later in range(group):
+                for early in range(later):
+                    same = places[early] == places[later]
+                    for side in range(len(outs)):
+                        totals[side][later] += jnp.where(same, added[side][early], 0.0)
             for side, out in enumerate(outs):
-                sums = []
-                for later in range(group):
-                    total = added[side][later]
-                    for early in range(later):
-                        total += jnp.where(places[early] == places[later], added[side][early], 0.0)
-                    sums.append(olds[side][later] + total)
-                for place, total in zip(places, sums):
-                    out[pl.ds(place, 1), :] = total
-            return carry
-
-        lax.fori_loop(0, lax.div(count + (group - 1), group), some, 0)
+                for place, old, total in zip(places, olds[side], totals[side]):
+                    out[pl.ds(place, 1), :] = old + total if sign > 0 else old - total
+            return fetch(index + 1)
+
+        lax.fori_loop(0, lax.div(count + (group - 1), group), some, fetch(0))
 
     def source_values(item):
         sign = (2 * src_signs[0, item] - 1).astype(jnp.float32)
         return sign * src_values[0, 0, item], sign * src_values[0, 1, item]
 
-    for copy in copies[:5]:
+    receivers, sources = rec_data.shape[-1], src_sign.shape[-1]
+    for copy in copies[:4]:
         copy.wait()
-    count = choose(lambda item: src_cells[0, item], src_cells.shape[1])
-    add(count, lambda item: src_cells[0, item], source_values, (first_buf, second_buf))
+    add(choose(receivers, sources), source_values, (first_buf, second_buf), 1)
+    copies[6].start()
     copies[7].start()
+    count = choose(0, receivers)
+    copies[4].wait()
+    copies[5].wait()
+    add(count, lambda item: (rec_values[0, 0, item], rec_values[0, 1, item]), (late_buf, now_buf), -1)
     copies[8].start()
-    count = choose(lambda item: rec_cells[item], rec_cells.shape[0])
-    copies[5].wait()
-    copies[6].wait()
-    add(
-        count, lambda item: rec_cells[item],
-        lambda item: (-rec_values[0, 0, item], -rec_values[0, 1, item]), (late_buf, now_buf),
-    )
     copies[9].start()
-    copies[10].start()
-    for copy in copies[7:]:
+    for copy in copies[6:]:
         copy.wait()
 
 
+GROUP = 4
+
+
+def cell_bits(size, width):
+    return (size + width - 1).bit_length()
+
+
 def inject(rec_cell, rec_data, src_cell, src_sign, wavelet, late, now):
+    size, width = math.prod(late.shape), late.shape[1]
+    bits = cell_bits(size, width)
+    receivers, sources = rec_cell.shape[0], src_cell.shape[1]
+    most = max(receivers, sources)
+    assert bits + (most - 1).bit_length() <= 31
+    items = np.concatenate([np.arange(receivers), np.arange(sources)]).astype(np.int32) << bits
+    local = jnp.concatenate([rec_cell, src_cell[0]]) - lax.axis_index("mp") * size
+    packed = jnp.where((local >= 0) & (local < size), local | items, -1)
     shape = jax.ShapeDtypeStruct(late.shape, jnp.float32)
-    most = max(rec_cell.shape[-1], src_cell.shape[-1])
-    small = (rec_cell, rec_data, src_cell, src_sign, wavelet)
+    padded = pltpu.VMEM((late.shape[0] + 8, width), jnp.float32)
+    small = (packed, rec_data, src_sign, wavelet)
     return pl.pallas_call(
         inject_kernel,
         out_shape=(shape,) * 4,
-        in_specs=[HBM] * 7,
+        in_specs=[HBM] * 6,
         out_specs=(HBM,) * 4,
-        scratch_shapes=[pltpu.VMEM(late.shape, jnp.float32)] * 4
+        scratch_shapes=[padded] * 4
         + [pltpu.SMEM(array.shape, array.dtype) for array in small]
-        + [pltpu.SMEM((most + 8,), jnp.int32), pltpu.SemaphoreType.DMA((11,))],
+        + [pltpu.SMEM((most + 2 * GROUP,), jnp.int32), pltpu.SemaphoreType.DMA((10,))],
         compiler_params=pltpu.CompilerParams(vmem_limit_bytes=VMEM_GRANT),
         name="inject",
     )(*small, late, now)
@@ -498,9 +514,18 @@
 
         for block in edges:
             pair_copy(block).start()
-        turn_start(0)
+
+        @pl.when(chip == lax.div(goal, 2))
+        def _():
+            turn_start(0)
+
         for block in edges:
             add_pair(block)
+
+        @pl.when(chip != lax.div(goal, 2))
+        def _():
+            turn_start(0)
+
         for block in edges:
             add_chips(block)
         turn_rows(0, REACH, parts[0])
@@ -603,27 +628,19 @@
 
 
 def mix_kernel(
-    raw_hbm, lined_hbm, planes_hbm, mix, raw_out, smooth, raw, lined, planes, buffer, sems
+    raw_hbm, lined, planes, mix, raw_out, smooth, raw, buffer, sems
 ):
     total_rows, others = lined.shape[0], planes.shape[0]
     wide = total_rows + others
     step = math.gcd(total_rows, 4)
     base = lax.axis_index("shot") * total_rows
-    copies = [
-        pltpu.make_async_copy(source, target, sems.at[index])
-        for index, (source, target) in enumerate(
-            [(lined_hbm, lined), (planes_hbm, planes), (raw_hbm, raw), (raw, raw_out)]
-        )
-    ]
-    for copy in copies[:3]:
-        copy.start()
-    for copy in copies[:3]:
-        copy.wait()
-    copies[3].start()
+    fetch = pltpu.make_async_copy(raw_hbm, raw, sems.at[0])
+    fetch.start()
+    store = pltpu.make_async_copy(raw, raw_out, sems.at[1])
 
     def write(index):
         here = pl.ds(index * step, step)
-        return pltpu.make_async_copy(buffer.at[here], smooth.at[here], sems.at[index + 4])
+        return pltpu.make_async_copy(buffer.at[here], smooth.at[here], sems.at[index + 2])
 
     def some(index, carry):
         totals = [None] * step
@@ -637,10 +654,12 @@
         write(index).start()
         return carry
 
+    fetch.wait()
+    store.start()
     lax.fori_loop(0, total_rows // step, some, 0)
     for index in range(total_rows // step):
         write(index).wait()
-    copies[3].wait()
+    store.wait()
 
 
 def mix_planes(raw, lined, planes, mix):
@@ -651,14 +670,13 @@
             jax.ShapeDtypeStruct(raw.shape, jnp.float32),
             jax.ShapeDtypeStruct(lined.shape, jnp.float32),
         ),
-        in_specs=[HBM, HBM, HBM, SMEM],
+        in_specs=[HBM, VMEM, VMEM, SMEM],
         out_specs=(HBM, HBM),
         scratch_shapes=[
             pltpu.VMEM(raw.shape, jnp.float32), pltpu.VMEM(lined.shape, jnp.float32),
-            pltpu.VMEM(planes.shape, jnp.float32), pltpu.VMEM(lined.shape, jnp.float32),
-            pltpu.SemaphoreType.DMA((steps + 4,)),
+            pltpu.SemaphoreType.DMA((steps + 2,)),
         ],
-        compiler_params=pltpu.CompilerParams(vmem_limit_bytes=VMEM_GRANT),
+        compiler_params=pltpu.CompilerParams(vmem_limit_bytes=MIX_GRANT),
         name="mix",
     )(raw, lined, planes, mix)
 
@@ -702,7 +720,8 @@
 
 
 VMEM_GRANT = 60 * 2**20
-GRADIENT_GRANT = 56 * 2**20
+GRADIENT_GRANT = 55 * 2**20
+MIX_GRANT = 56 * 2**20
 
 
 def solution(mesh):

time: 103 us -> 103 us (level)
  other arithmetic: 0 us -> 1.34 us
    pallas_call x1, Pallas kernels: 17.1 us -> 15.2 us  [inject(): pl.pallas_call(inject_kernel, out_shape=(shape,) * 4, in_specs=[HBM] * 6,...]
    select_n x0 -> x1, other arithmetic: none -> 1.34 us  [inject(): packed = jnp.where((local >= 0) & (local < size), local | items, -1)]
where the time goes in v2:
time: 103 us
  Pallas kernels  101 us (98%)
  other arithmetic  1.34 us (1%)
    pallas_call x1, Pallas kernels, per_device(): pl.pallas_call(kernel, out_shape=outs, in_specs=[HBM] * 8 + [VMEM] * 4 +...  80.9 us
    pallas_call x1, Pallas kernels, inject(): pl.pallas_call(inject_kernel, out_shape=(shape,) * 4, in_specs=[HBM] * 6,...  15.2 us
    pallas_call x1, Pallas kernels, mix_planes(): pl.pallas_call(mix_kernel, out_shape=(jax.ShapeDtypeStruct(raw.shape, jnp...  4.58 us

profile of v2, /device:TPU:0, one launch (start us, length us, event | category | flops | bytes accessed | tf_op | source)
XLA Modules:
  0.0 102.8 jit_solution(6940539122604019745)
XLA Ops:
  0.6 1.3 %or_select_fusion.packed = s32[2112]{0:T(1024)} fusion(s32[2112]{0:T(1024)} %constant.26.clone, s32[64]{0:T(128)} %bitcast.20, s32[2048]{0:T(1024)} %param.25, s32[]{:T(128)S(6)} %mul.3), kind=kLoop, calls=%fused_computation.1 | loop fusion | flops 14784 | bytes 25348 | tf_op jit(solution)/shard_map/jit(_where)/select_n | solution.py:173
  2.0 15.2 %inject.1 = (f32[6144,128]{1,0:T(8,128)}, f32[6144,128]{1,0:T(8,128)}, f32[6144,128]{1,0:T(8,128)}, f32[6144,128]{1,0:T(8,128)}) custom-call(s32[2112]{0:T(1024)} %or_select_fusion.packed, f32[1,2,2048]{2,1,0:T(2,128)} %rec_data.1, s32[1,64]{1,0:T(1,128)} %src_sign.1, f32[1,2,64]{2,1,0:T(2,128)} %wavelet.1, f32[6144,128]{1,0:T(8,128)} %bitcast.19, ...), custom_call_target="tpu_custom_call" | custom-call | tf_op jit(solution)/shard_map/inject/pallas_call | solution.py:177
  17.2 80.9 %gradient.1 = (f32[24,64,128]{2,1,0:T(8,128)}, f32[24,32,256]{2,1,0:T(8,128)}, f32[3,32,256]{2,1,0:T(8,128)}) custom-call(f32[24,256,128]{2,1,0:T(8,128)} %bitcast.13, f32[24,256,128]{2,1,0:T(8,128)} %bitcast.12, f32[24,256,128]{2,1,0:T(8,128)} %bitcast.14, f32[24,256,128]{2,1,0:T(8,128)} %courant_hbm.1, f32[24,256,128]{2,1,0:T(8,128)} %bitcast.15, ...), custom_call_target="tpu_custom_call" | custom-call | tf_op jit(solution)/shard_map/gradient/pallas_call | solution.py:701
  98.1 4.6 %mix.2 = (f32[24,64,128]{2,1,0:T(8,128)}, f32[24,32,256]{2,1,0:T(8,128)}) custom-call(f32[24,64,128]{2,1,0:T(8,128)} %get-tuple-element.15.raw_hbm, f32[24,32,256]{2,1,0:T(8,128)} %get-tuple-element.16.lined, f32[3,32,256]{2,1,0:T(8,128)} %get-tuple-element.17.planes, f32[2592]{0:T(1024)} %constant.27.clone.mix), custom_call_target="tpu_custom_call" | custom-call | tf_op jit(solution)/shard_map/mix/pallas_call | solution.py:667

commit v3 on v2

--- a/solution.py
+++ b/solution.py
@@ -91,7 +91,7 @@
     group = GROUP
 
     def choose(start, total):
-        together = math.gcd(total, 32)
+        together = math.gcd(total, 8)
 
         def some(index, count):
             values = [cells[start + index * together + extra] for extra in range(together)]
@@ -514,18 +514,9 @@
 
         for block in edges:
             pair_copy(block).start()
-
-        @pl.when(chip == lax.div(goal, 2))
-        def _():
-            turn_start(0)
-
+        turn_start(0)
         for block in edges:
             add_pair(block)
-
-        @pl.when(chip != lax.div(goal, 2))
-        def _():
-            turn_start(0)
-
         for block in edges:
             add_chips(block)
         turn_rows(0, REACH, parts[0])
@@ -654,9 +645,11 @@
         write(index).start()
         return carry
 
+    half = total_rows // step // 2
+    lax.fori_loop(0, half, some, 0)
     fetch.wait()
     store.start()
-    lax.fori_loop(0, total_rows // step, some, 0)
+    lax.fori_loop(half, total_rows // step, some, 0)
     for index in range(total_rows // step):
         write(index).wait()
     store.wait()

time: 103 us -> 102 us (level)
  Pallas kernels: 101 us -> 99.7 us
where the time goes in v3:
time: 102 us
  Pallas kernels  99.7 us (98%)
  other arithmetic  1.34 us (1%)
    pallas_call x1, Pallas kernels, per_device(): pl.pallas_call(kernel, out_shape=outs, in_specs=[HBM] * 8 + [VMEM] * 4 +...  80.4 us
    pallas_call x1, Pallas kernels, inject(): pl.pallas_call(inject_kernel, out_shape=(shape,) * 4, in_specs=[HBM] * 6,...  15.5 us
    pallas_call x1, Pallas kernels, mix_planes(): pl.pallas_call(mix_kernel, out_shape=(jax.ShapeDtypeStruct(raw.shape, jnp...  3.8 us

profile of v3, /device:TPU:0, one launch (start us, length us, event | category | flops | bytes accessed | tf_op | source)
XLA Modules:
  0.0 101.8 jit_solution(560219379188308606)
XLA Ops:
  0.6 1.3 %or_select_fusion.packed = s32[2112]{0:T(1024)} fusion(s32[2112]{0:T(1024)} %constant.26.clone, s32[64]{0:T(128)} %bitcast.20, s32[2048]{0:T(1024)} %param.25, s32[]{:T(128)S(6)} %mul.3), kind=kLoop, calls=%fused_computation.1 | loop fusion | flops 14784 | bytes 25348 | tf_op jit(solution)/shard_map/jit(_where)/select_n | solution.py:173
  2.0 15.5 %inject.1 = (f32[6144,128]{1,0:T(8,128)}, f32[6144,128]{1,0:T(8,128)}, f32[6144,128]{1,0:T(8,128)}, f32[6144,128]{1,0:T(8,128)}) custom-call(s32[2112]{0:T(1024)} %or_select_fusion.packed, f32[1,2,2048]{2,1,0:T(2,128)} %rec_data.1, s32[1,64]{1,0:T(1,128)} %src_sign.1, f32[1,2,64]{2,1,0:T(2,128)} %wavelet.1, f32[6144,128]{1,0:T(8,128)} %bitcast.19, ...), custom_call_target="tpu_custom_call" | custom-call | tf_op jit(solution)/shard_map/inject/pallas_call | solution.py:177
  17.4 80.4 %gradient.1 = (f32[24,64,128]{2,1,0:T(8,128)}, f32[24,32,256]{2,1,0:T(8,128)}, f32[3,32,256]{2,1,0:T(8,128)}) custom-call(f32[24,256,128]{2,1,0:T(8,128)} %bitcast.13, f32[24,256,128]{2,1,0:T(8,128)} %bitcast.12, f32[24,256,128]{2,1,0:T(8,128)} %bitcast.14, f32[24,256,128]{2,1,0:T(8,128)} %courant_hbm.1, f32[24,256,128]{2,1,0:T(8,128)} %bitcast.15, ...), custom_call_target="tpu_custom_call" | custom-call | tf_op jit(solution)/shard_map/gradient/pallas_call | solution.py:694
  97.9 3.8 %mix.2 = (f32[24,64,128]{2,1,0:T(8,128)}, f32[24,32,256]{2,1,0:T(8,128)}) custom-call(f32[24,64,128]{2,1,0:T(8,128)} %get-tuple-element.15.raw_hbm, f32[24,32,256]{2,1,0:T(8,128)} %get-tuple-element.16.lined, f32[3,32,256]{2,1,0:T(8,128)} %get-tuple-element.17.planes, f32[2592]{0:T(1024)} %constant.27.clone.mix), custom_call_target="tpu_custom_call" | custom-call | tf_op jit(solution)/shard_map/mix/pallas_call | solution.py:660

commit v4 on v3

--- a/solution.py
+++ b/solution.py
@@ -13,7 +13,7 @@
 COEFS = (8.0 / 5.0, -1.0 / 5.0, 8.0 / 315.0, -1.0 / 560.0)
 CENTER = -205.0 / 72.0
 REACH = 4
-HIGHEST = lax.Precision.HIGHEST
+HIGHEST = lax.Precision.HIGH
 MESH = pl.DeviceIdType.MESH
 
 SCALE = 5040.0

time: 102 us -> 102 us (level)
  no operation moved by 1% of the time
where the time goes in v4:
time: 102 us; the launch traced here: 101 us
  Pallas kernels  99.1 us (97%)
  other arithmetic  1.34 us (1%)
    pallas_call x1, Pallas kernels, per_device(): pl.pallas_call(kernel, out_shape=outs, in_specs=[HBM] * 8 + [VMEM] * 4 +...  80 us
    pallas_call x1, Pallas kernels, inject(): pl.pallas_call(inject_kernel, out_shape=(shape,) * 4, in_specs=[HBM] * 6,...  15.3 us
    pallas_call x1, Pallas kernels, mix_planes(): pl.pallas_call(mix_kernel, out_shape=(jax.ShapeDtypeStruct(raw.shape, jnp...  3.8 us

profile of v4, /device:TPU:0, one launch (start us, length us, event | category | flops | bytes accessed | tf_op | source)
XLA Modules:
  0.0 101.3 jit_solution(10261227581488417976)
XLA Ops:
  0.6 1.3 %or_select_fusion.packed = s32[2112]{0:T(1024)} fusion(s32[2112]{0:T(1024)} %constant.26.clone, s32[64]{0:T(128)} %bitcast.20, s32[2048]{0:T(1024)} %param.25, s32[]{:T(128)S(6)} %mul.3), kind=kLoop, calls=%fused_computation.1 | loop fusion | flops 14784 | bytes 25348 | tf_op jit(solution)/shard_map/jit(_where)/select_n | solution.py:173
  2.0 15.3 %inject.1 = (f32[6144,128]{1,0:T(8,128)}, f32[6144,128]{1,0:T(8,128)}, f32[6144,128]{1,0:T(8,128)}, f32[6144,128]{1,0:T(8,128)}) custom-call(s32[2112]{0:T(1024)} %or_select_fusion.packed, f32[1,2,2048]{2,1,0:T(2,128)} %rec_data.1, s32[1,64]{1,0:T(1,128)} %src_sign.1, f32[1,2,64]{2,1,0:T(2,128)} %wavelet.1, f32[6144,128]{1,0:T(8,128)} %bitcast.19, ...), custom_call_target="tpu_custom_call" | custom-call | tf_op jit(solution)/shard_map/inject/pallas_call | solution.py:177
  17.3 80.0 %gradient.1 = (f32[24,64,128]{2,1,0:T(8,128)}, f32[24,32,256]{2,1,0:T(8,128)}, f32[3,32,256]{2,1,0:T(8,128)}) custom-call(f32[24,256,128]{2,1,0:T(8,128)} %bitcast.13, f32[24,256,128]{2,1,0:T(8,128)} %bitcast.12, f32[24,256,128]{2,1,0:T(8,128)} %bitcast.14, f32[24,256,128]{2,1,0:T(8,128)} %courant_hbm.1, f32[24,256,128]{2,1,0:T(8,128)} %bitcast.15, ...), custom_call_target="tpu_custom_call" | custom-call | tf_op jit(solution)/shard_map/gradient/pallas_call | solution.py:694
  97.3 3.8 %mix.2 = (f32[24,64,128]{2,1,0:T(8,128)}, f32[24,32,256]{2,1,0:T(8,128)}) custom-call(f32[24,64,128]{2,1,0:T(8,128)} %get-tuple-element.15.raw_hbm, f32[24,32,256]{2,1,0:T(8,128)} %get-tuple-element.16.lined, f32[3,32,256]{2,1,0:T(8,128)} %get-tuple-element.17.planes, f32[2592]{0:T(1024)} %constant.27.clone.mix), custom_call_target="tpu_custom_call" | custom-call | tf_op jit(solution)/shard_map/mix/pallas_call | solution.py:660
